TPU v7x, 256 devices: a whole 4x4x8 slice. The times are simulated.
256 devices in a mesh: dp: 32 (over z_lo, y, core), tensor: 8 (over x, z_hi).
Axes of the slice: x: 4, y: 4, z: 8 (z_hi: 2, z_lo: 4; z = z_hi * 4 + z_lo), core: 2. Of those that a mesh axis runs over, the one named last changes fastest.
Arguments:
- tokens: bfloat16 [8192, 8192], P(('dp', 'tensor')), may hold values from -6 to 6
- gain: float32 [8192], replicated, may hold values from 0.1 to 1.9
- stale: bfloat16 [8192, 2048], P(None, 'tensor'), may hold values from -0.0625 to 0.0625
- bias: float32 [2048], P('tensor'), may hold values from -3 to 3
- first: float32 [8192, 2048], P(('dp', 'tensor')), may hold values from -6 to 6
- second: float32 [8192, 2048], P(('dp', 'tensor')), may hold values from 0.1 to 10
- grad: float32 [8192, 2048], P(('dp', 'tensor')), may hold values from -6 to 6
- residual: float32 [8192, 2048], P(('dp', 'tensor')), may hold values from -0.12 to 0.12
- exponent: int32 [256, 16], P(('dp', 'tensor')), may hold values from 10 to 17
Outputs:
- new_first: float32 [8192, 2048], P(('dp', 'tensor'))
- new_second: float32 [8192, 2048], P(('dp', 'tensor'))
- projected: bfloat16 [8192, 2048], P('dp', 'tensor')
All inputs are finite; a program needn't handle non-finite values.
Results may differ from a plain program's by a relative error of at most 0.0062.
Values may be sent and summed in bfloat16 or wider, within the bound.
A program may use at most 128 MiB of HBM per device.

v0:
```python
import jax
import jax.numpy as jnp
from jax import lax
from jax.sharding import PartitionSpec as P

QROWS = 32
QCOL = 128


def on_device(tokens, gain, stale, bias, first, second, grad, residual, exponent):
    values = tokens.astype(jnp.float32)
    meansq = jnp.mean(values * values, axis=1, keepdims=True)
    normed = (values * lax.rsqrt(meansq + 1e-06) * gain[None, :]).astype(jnp.bfloat16)
    whole = lax.all_gather(normed, "tensor", axis=0, tiled=True)
    new_first = 0.9 * first + 0.1 * grad
    new_second = 0.95 * second + 0.05 * grad * grad
    corrected = 0.02 * new_first / (jnp.sqrt(new_second) + 1e-08) + residual
    expo = exponent.astype(jnp.float32)
    upward = jnp.exp2(expo)[:, None, :, None]
    downward = jnp.exp2(-expo)[:, None, :, None]
    local_rows = first.shape[0]
    full_cols = first.shape[1]
    blocked = corrected.reshape(exponent.shape[0], QROWS, exponent.shape[1], QCOL) * upward
    quant = jnp.clip(blocked, -448.0, 448.0).astype(jnp.bfloat16)
    quant = lax.optimization_barrier(quant)
    delta = (
        (quant.astype(jnp.float32) * downward).reshape(local_rows, full_cols).astype(jnp.bfloat16)
    )
    head_cols = stale.shape[1]
    gathered = lax.all_gather(delta, "dp", axis=0, tiled=True)
    spread = lax.all_to_all(gathered, "tensor", split_axis=1, concat_axis=0, tiled=True)
    tensor_count = lax.axis_size("tensor")
    replica_count = lax.axis_size("dp")
    ordered = spread.reshape(tensor_count, replica_count, local_rows, head_cols)
    ordered = ordered.transpose(1, 0, 2, 3).reshape(stale.shape[0], head_cols)
    merged = (stale.astype(jnp.float32) + ordered.astype(jnp.float32)).astype(jnp.bfloat16)
    product = jnp.dot(whole, merged, preferred_element_type=jnp.float32)
    projected = (product + bias[None, :]).astype(jnp.bfloat16)
    return (new_first, new_second, projected)


def solution(mesh):
    return jax.shard_map(
        on_device,
        mesh=mesh,
        in_specs=(
            P(("dp", "tensor"), None),
            P(),
            P(None, "tensor"),
            P("tensor"),
            P(("dp", "tensor"), None),
            P(("dp", "tensor"), None),
            P(("dp", "tensor"), None),
            P(("dp", "tensor"), None),
            P(("dp", "tensor"), None),
        ),
        out_specs=(P(("dp", "tensor"), None), P(("dp", "tensor"), None), P("dp", "tensor")),
        check_vma=False,
    )
```

profile of v0, /device:TPU:1, one launch (start us, length us, event | category | flops | bytes accessed | tf_op | source)
XLA Modules:
  0.0 273.7 jit_solution(1441821206613189198)
XLA Ops:
  8.0 0.0 all-gather.5.cloned.1.call-start
  8.0 2.1 add_bitcast_fusion
  10.2 0.7 exponential_bitcast_fusion
  10.9 0.1 fusion.7
  11.0 0.1 multiply_convert_fusion
  11.1 0.7 copy.21
  11.8 0.0 all-gather.5.cloned.1.call-update
  11.8 66.8 %all-gather.5.cloned.1.call-done = bf16[1024,2048]{1,0:T(8,128)(2,1)} async-done(((bf16[32,2048]{1,0:T(8,128)(2,1)}), bf16[1024,2048]{1,0:T(8,128)(2,1)}) %all-gather.5.cloned.1.call-update) | async-done | bytes 4194320 | tf_op jit(solution)/shard_map/all_gather | solution.py:30
  78.6 6.4 %copy.15 = bf16[1024,2048]{0,1:T(8,128)(2,1)} copy(bf16[1024,2048]{1,0:T(8,128)(2,1)} %all-gather.5.cloned.1.call-done) | data formatting | bytes 8388608 | tf_op jit(solution)/shard_map/all_gather | solution.py:30
  85.0 0.0 copy-start.1
  85.0 0.0 copy-start.2
  85.0 7.9 %all-to-all-start = ((bf16[1024,8,256]{0,2,1:T(8,128)(2,1)}), bf16[1024,8,256]{0,2,1:T(8,128)(2,1)}, u32[]{:S(2)}, u32[]{:S(2)}) async-start(bf16[1024,8,256]{0,2,1:T(8,128)(2,1)} %bitcast.32), calls=%async_computation | async-start | bytes 8388608 | tf_op jit(solution)/shard_map/all_to_all | solution.py:31
  92.9 0.0 all-gather.3.cloned.1.call-start
  93.0 0.0 copy-done.1
  93.0 0.2 fusion.2
  93.2 0.0 copy-done.2
  93.2 1.0 fusion.4
  94.2 0.0 all-gather.3.cloned.1.call-update
  94.3 78.9 %all-to-all-done = bf16[1024,8,256]{0,2,1:T(8,128)(2,1)} async-done(((bf16[1024,8,256]{0,2,1:T(8,128)(2,1)}), bf16[1024,8,256]{0,2,1:T(8,128)(2,1)}, u32[]{:S(2)}, u32[]{:S(2)}) %all-to-all-start) | async-done | bytes 4194336 | tf_op jit(solution)/shard_map/all_to_all | solution.py:31
  173.2 6.5 %convert_bitcast_fusion = f32[8,1024,256]{1,2,0:T(8,128)} fusion(bf16[1024,8,256]{0,2,1:T(8,128)(2,1)} %all-to-all-done), kind=kLoop, calls=%fused_computation.2 | loop fusion | flops 2097152 | bytes 12582912 | tf_op jit(solution)/shard_map/convert_element_type | solution.py:36
  179.6 9.1 %copy.16 = f32[8,1024,256]{2,1,0:T(8,128)} copy(f32[8,1024,256]{1,2,0:T(8,128)} %convert_bitcast_fusion) | data formatting | bytes 16777216 | tf_op jit(solution)/shard_map/convert_element_type | solution.py:36
  188.8 0.0 copy-start
  188.8 4.4 %copy.17 = f32[32,8,32,256]{3,2,1,0:T(8,128)S(1)} copy(f32[32,8,32,256]{3,2,0,1:T(8,128)} %bitcast.31) | data formatting | bytes 16777216 | tf_op jit(solution)/shard_map/convert_element_type | solution.py:36
  193.2 0.2 copy-done
  193.4 0.0 copy-start.3
  193.4 3.4 %fusion = bf16[8192,256]{1,0:T(8,128)(2,1)} fusion(f32[32,8,32,256]{3,2,1,0:T(8,128)S(1)} %copy.17, bf16[8192,256]{1,0:T(8,128)(2,1)S(1)} %copy-done), kind=kLoop, calls=%fused_computation.1 | loop fusion | flops 6291456 | bytes 16777216 | tf_op jit(solution)/shard_map/convert_element_type | solution.py:36
  196.8 64.1 %all-gather.3.cloned.1.call-done = bf16[256,8192]{1,0:T(8,128)(2,1)} async-done(((bf16[32,8192]{1,0:T(8,128)(2,1)}), bf16[256,8192]{1,0:T(8,128)(2,1)}) %all-gather.3.cloned.1.call-update) | async-done | bytes 4194320 | tf_op jit(solution)/shard_map/all_gather | solution.py:14
  260.9 0.0 copy-done.3
  260.9 5.4 %fusion.1 = bf16[256,256]{1,0:T(8,128)(2,1)} fusion(bf16[256,8192]{1,0:T(8,128)(2,1)} %all-gather.3.cloned.1.call-done, bf16[8192,256]{1,0:T(8,128)(2,1)} %fusion, f32[256]{0:T(256)S(1)} %copy-done.3), kind=kOutput, calls=%fused_computation.6 | convolution fusion | flops 1073872896 | bytes 8520704 | tf_op jit(solution)/shard_map/dot_general | solution.py:37
  (2 shorter events, 0.1 us)
Async XLA Ops:
  8.0 70.6 %all-gather.5.cloned.1.call-start = ((), (), s32[]{:S(2)}) async-start(), calls=%async_computation.2 | async-start | bytes 4325376 | tf_op jit(solution)/shard_map/all_gather | solution.py:30
  85.0 8.0 %copy-start.1 = (bf16[32,8192]{1,0:T(8,128)(2,1)S(1)}, bf16[32,8192]{1,0:T(8,128)(2,1)}, u32[]{:S(2)}) copy-start(bf16[32,8192]{1,0:T(8,128)(2,1)} %param.9) | copy-start | bytes 1572868
  85.0 8.2 %copy-start.2 = (f32[8192]{0:T(1024)S(1)}, f32[8192]{0:T(1024)}, u32[]{:S(2)}) copy-start(f32[8192]{0:T(1024)} %param.10) | copy-start | bytes 98308
  85.0 88.2 %all-to-all-start = ((bf16[1024,8,256]{0,2,1:T(8,128)(2,1)}), bf16[1024,8,256]{0,2,1:T(8,128)(2,1)}, u32[]{:S(2)}, u32[]{:S(2)}) async-start(bf16[1024,8,256]{0,2,1:T(8,128)(2,1)} %bitcast.32), calls=%async_computation | async-start | bytes 8388608 | tf_op jit(solution)/shard_map/all_to_all | solution.py:31
  92.9 167.9 %all-gather.3.cloned.1.call-start = ((), (), s32[]{:S(2)}) async-start(), calls=%async_computation.1 | async-start | bytes 4718592 | tf_op jit(solution)/shard_map/all_gather | solution.py:14
  188.8 4.6 %copy-start = (bf16[8192,256]{1,0:T(8,128)(2,1)S(1)}, bf16[8192,256]{1,0:T(8,128)(2,1)}, u32[]{:S(2)}) copy-start(bf16[8192,256]{1,0:T(8,128)(2,1)} %param.11) | copy-start | bytes 12582916
  193.4 67.5 %copy-start.3 = (f32[256]{0:T(256)S(1)}, f32[256]{0:T(256)}, u32[]{:S(2)}) copy-start(f32[256]{0:T(256)} %param.12) | copy-start | bytes 3076
Sparse Core Ops, SparseCore 0:
  11.9 66.6 all-gather.4
Sparse Core Ops, SparseCore 1:
  96.0 164.8 all-gather.2
where the time goes:
time: 274 us
  waiting for transfers between devices  210 us (77%)
  local copies, waits for them, and re-layouts  20.8 us (8%)
  between operations  15.5 us (6%)
  other arithmetic  14.1 us (5%)
  starting transfers between devices  7.99 us (3%)
  matrix products  5.37 us (2%)
    all_to_all x1, waiting for transfers between devices, on_device(): lax.all_to_all(gathered, 'tensor', split_axis=1, concat_axis=0, tiled=True)  78.9 us
    all_gather x1, waiting for transfers between devices, on_device(): gathered = lax.all_gather(delta, 'dp', axis=0, tiled=True)  66.8 us
    all_gather x1, waiting for transfers between devices, on_device(): whole = lax.all_gather(normed, 'tensor', axis=0, tiled=True)  64.1 us
    convert_element_type x2, local copies, waits for them, and re-layouts, on_device(): ordered.astype(jnp.float32)  13.5 us
    all_to_all x1, starting transfers between devices, on_device(): lax.all_to_all(gathered, 'tensor', split_axis=1, concat_axis=0, tiled=True)  7.92 us
    convert_element_type x1, other arithmetic, on_device(): ordered.astype(jnp.float32)  6.46 us
    all_gather x1, local copies, waits for them, and re-layouts, on_device(): gathered = lax.all_gather(delta, 'dp', axis=0, tiled=True)  6.38 us
  transfers between devices with their start and end apart: 3, of which 3 were waited for; matrix products, arithmetic and copies ran while one was open for 9% of the time, Pallas kernels for 0%

commit v1 on v0

--- a/solution.py
+++ b/solution.py
@@ -27,7 +27,9 @@
         (quant.astype(jnp.float32) * downward).reshape(local_rows, full_cols).astype(jnp.bfloat16)
     )
     head_cols = stale.shape[1]
-    gathered = lax.all_gather(delta, "dp", axis=0, tiled=True)
+    gathered = jnp.concatenate(
+        lax.all_to_all(jnp.stack([delta] * lax.axis_size("dp")), "dp", 0, 0), axis=0
+    )
     spread = lax.all_to_all(gathered, "tensor", split_axis=1, concat_axis=0, tiled=True)
     tensor_count = lax.axis_size("tensor")
     replica_count = lax.axis_size("dp")

time: 274 us -> 303 us (1.11)
  blocking collectives: 0 us -> 104 us
  waiting for transfers between devices: 210 us -> 153 us
  local copies, waits for them, and re-layouts: 20.8 us -> 7.06 us
  other arithmetic: 14.1 us -> 10.8 us
    all_to_all x0 -> x1, blocking collectives: none -> 104 us  [on_device(): lax.all_to_all(jnp.stack([delta] * lax.axis_size('dp')), 'dp', 0, 0)]
    all_gather x1 -> x0, waiting for transfers between devices: 66.8 us -> none  [on_device(): gathered = lax.all_gather(delta, 'dp', axis=0, tiled=True)]
    all_gather x1, waiting for transfers between devices: 64.1 us -> 76.1 us  [on_device(): whole = lax.all_gather(normed, 'tensor', axis=0, tiled=True)]
    convert_element_type x2 -> x1, local copies, waits for them, and re-layouts: 13.5 us -> 1.65 us  [on_device(): ordered.astype(jnp.float32)]
    all_gather x1 -> x0, local copies, waits for them, and re-layouts: 6.38 us -> none  [on_device(): gathered = lax.all_gather(delta, 'dp', axis=0, tiled=True)]
    convert_element_type x1, other arithmetic: 6.46 us -> 2.94 us  [on_device(): ordered.astype(jnp.float32)]
  transfers between devices with their start and end apart: 3 -> 2, of which waited for: 3 -> 2; matrix products, arithmetic and copies ran while one was open for 9% -> 3% of each run, Pallas kernels for 0% -> 0%
where the time goes in v1:
time: 303 us
  waiting for transfers between devices  153 us (50%)
  blocking collectives  104 us (34%)
  between operations  14.1 us (5%)
  other arithmetic  10.8 us (4%)
  starting transfers between devices  8.12 us (3%)
  local copies, waits for them, and re-layouts  7.06 us (2%)
  matrix products  5.37 us (2%)
    all_to_all x1, blocking collectives, on_device(): lax.all_to_all(jnp.stack([delta] * lax.axis_size('dp')), 'dp', 0, 0)  104 us
    all_to_all x1, waiting for transfers between devices, on_device(): lax.all_to_all(gathered, 'tensor', split_axis=1, concat_axis=0, tiled=True)  77 us
    all_gather x1, waiting for transfers between devices, on_device(): whole = lax.all_gather(normed, 'tensor', axis=0, tiled=True)  76.1 us
    all_to_all x1, starting transfers between devices, on_device(): lax.all_to_all(gathered, 'tensor', split_axis=1, concat_axis=0, tiled=True)  8.08 us
  transfers between devices with their start and end apart: 2, of which 2 were waited for; matrix products, arithmetic and copies ran while one was open for 3% of the time, Pallas kernels for 0%

profile of v1, /device:TPU:1, one launch (start us, length us, event | category | flops | bytes accessed | tf_op | source)
XLA Modules:
  0.0 302.6 jit_solution(16419157968157197992)
XLA Ops:
  7.2 2.1 add_bitcast_fusion
  9.3 0.7 exponential_bitcast_fusion
  10.0 0.1 fusion.7
  10.1 0.1 multiply_convert_fusion
  10.3 0.5 stack.2
  10.8 104.0 %all_to_all.18 = bf16[32,32,2048]{2,1,0:T(8,128)(2,1)S(1)} all-to-all(bf16[32,32,2048]{2,1,0:T(8,128)(2,1)S(1)} %stack.2), channel_id=1, replica_groups=mesh['dp'=32,'tensor'=8] {'dp'}, dimensions={0} | all-to-all | bytes 8388608 | tf_op jit(solution)/shard_map/all_to_all | solution.py:31
  114.8 1.5 copy.18
  116.3 2.8 copy.14
  119.1 0.0 copy-start.1
  119.1 0.0 copy-start.2
  119.1 8.1 %all-to-all-start.1 = ((bf16[1024,8,256]{2,0,1:T(8,128)(2,1)}), bf16[1024,8,256]{2,0,1:T(8,128)(2,1)}, u32[]{:S(2)}, u32[]{:S(2)}) async-start(bf16[1024,8,256]{2,0,1:T(8,128)(2,1)} %copy.14), calls=%async_computation.1 | async-start | bytes 8388608 | tf_op jit(solution)/shard_map/all_to_all | solution.py:33
  127.2 0.0 all-gather.2.cloned.1.call-start
  127.2 0.0 copy-done.1
  127.2 0.2 fusion.2
  127.5 0.0 copy-done.2
  127.5 1.0 fusion.4
  128.5 0.0 all-gather.2.cloned.1.call-update
  128.5 77.0 %all-to-all-done.1 = bf16[1024,8,256]{2,0,1:T(8,128)(2,1)} async-done(((bf16[1024,8,256]{2,0,1:T(8,128)(2,1)}), bf16[1024,8,256]{2,0,1:T(8,128)(2,1)}, u32[]{:S(2)}, u32[]{:S(2)}) %all-to-all-start.1) | async-done | bytes 4194336 | tf_op jit(solution)/shard_map/all_to_all | solution.py:33
  205.5 2.9 convert_element_type.73
  208.5 0.0 copy-start
  208.5 1.7 copy.15
  210.2 0.5 copy-done
  210.7 0.0 copy-start.3
  210.7 3.6 %fusion = bf16[8192,256]{1,0:T(8,128)(2,1)} fusion(f32[32,8,32,256]{3,2,1,0:T(8,128)S(1)} %copy.15, bf16[8192,256]{1,0:T(8,128)(2,1)S(1)} %copy-done), kind=kLoop, calls=%fused_computation.1 | loop fusion | flops 6291456 | bytes 16777216 | tf_op jit(solution)/shard_map/convert_element_type | solution.py:38
  214.3 76.1 %all-gather.2.cloned.1.call-done = bf16[256,8192]{1,0:T(8,128)(2,1)} async-done(((bf16[32,8192]{1,0:T(8,128)(2,1)}), bf16[256,8192]{1,0:T(8,128)(2,1)}) %all-gather.2.cloned.1.call-update) | async-done | bytes 4194320 | tf_op jit(solution)/shard_map/all_gather | solution.py:14
  290.4 0.0 copy-done.3
  290.4 5.4 %fusion.1 = bf16[256,256]{1,0:T(8,128)(2,1)} fusion(bf16[256,8192]{1,0:T(8,128)(2,1)} %all-gather.2.cloned.1.call-done, bf16[8192,256]{1,0:T(8,128)(2,1)} %fusion, f32[256]{0:T(256)S(1)} %copy-done.3), kind=kOutput, calls=%fused_computation.5 | convolution fusion | flops 1073872896 | bytes 8520704 | tf_op jit(solution)/shard_map/dot_general | solution.py:39
  (3 shorter events, 0.1 us)
Async XLA Ops:
  119.1 8.1 %copy-start.1 = (bf16[32,8192]{1,0:T(8,128)(2,1)S(1)}, bf16[32,8192]{1,0:T(8,128)(2,1)}, u32[]{:S(2)}) copy-start(bf16[32,8192]{1,0:T(8,128)(2,1)} %param.9) | copy-start | bytes 1572868
  119.1 8.4 %copy-start.2 = (f32[8192]{0:T(1024)S(1)}, f32[8192]{0:T(1024)}, u32[]{:S(2)}) copy-start(f32[8192]{0:T(1024)} %param.10) | copy-start | bytes 98308
  119.1 86.4 %all-to-all-start.1 = ((bf16[1024,8,256]{2,0,1:T(8,128)(2,1)}), bf16[1024,8,256]{2,0,1:T(8,128)(2,1)}, u32[]{:S(2)}, u32[]{:S(2)}) async-start(bf16[1024,8,256]{2,0,1:T(8,128)(2,1)} %copy.14), calls=%async_computation.1 | async-start | bytes 8388608 | tf_op jit(solution)/shard_map/all_to_all | solution.py:33
  127.2 163.2 %all-gather.2.cloned.1.call-start = ((), (), s32[]{:S(2)}) async-start(), calls=%async_computation.2 | async-start | bytes 4718592 | tf_op jit(solution)/shard_map/all_gather | solution.py:14
  208.5 2.2 copy-start
  210.7 79.7 %copy-start.3 = (f32[256]{0:T(256)S(1)}, f32[256]{0:T(256)}, u32[]{:S(2)}) copy-start(f32[256]{0:T(256)} %param.12) | copy-start | bytes 3076
Sparse Core Ops, SparseCore 0:
  130.6 159.7 all-gather.1
